TPU v7x, 512 devices: a whole 4x8x8 slice. The times are simulated.
512 devices in a mesh: term: 8 (over z), sector: 64 (over x, y, core).
Axes of the slice: x: 4, y: 8, z: 8, core: 2. Of those that a mesh axis runs over, the one named last changes fastest.
Arguments:
- wave_tiles: bfloat16 [1024, 2, 128, 128], P('sector'), may hold values from -6 to 6
- left_env: bfloat16 [8, 64, 128, 128], P('term', 'sector'), may hold values from -0.5 to 0.5
- right_env: bfloat16 [8, 64, 128, 128], P('term', 'sector'), may hold values from -0.5 to 0.5
- send_list: int32 [64, 128], P('sector'), may hold values from -1 to 15, as said below
- left_tasks: int32 [8, 64, 96, 3], P('term', 'sector'), may hold values from 0 to 127, as said below
- right_tasks: int32 [8, 64, 256, 3], P('term', 'sector'), may hold values from 0 to 63, as said below
Outputs:
- sigma: float32 [1024, 2, 128, 128], P('sector', None, 'term')
Inputs may be any that keep to these rules, and one draw needn't show every extreme that they name: send_list[s, o * 2 + c] is a tile index local to sender s, or -1 for an empty slot; some owner drawn from the seed receives a full 2 tiles from every sender. `left_tasks`: entries 0, 1, 2 lie below 64, 128 and 32. `right_tasks`: entries 0, 1, 2 lie below 32, 64 and 16.
All inputs are finite; a program needn't handle non-finite values.
Results may differ from a plain program's by a relative error of at most 0.0029.
Values may be sent and summed in bfloat16 or wider, within the bound.
A program may use at most 128 MiB of HBM per device.

v0:
```python
import math
import jax
import jax.numpy as jnp
from jax import lax
from jax.sharding import PartitionSpec as P

INTER_TILES = 32


def run_tasks(tasks, first_tiles, second_tiles, contract, count):
    block = math.gcd(tasks.shape[0], 32)
    shape = (count,) + tuple(contract(first_tiles[:1], second_tiles[:1]).shape[1:])

    def step(turn, total):
        rows = lax.dynamic_slice_in_dim(tasks, turn * block, block, 0)
        first = jnp.take(first_tiles, rows[:, 0], axis=0)
        second = jnp.take(second_tiles, rows[:, 1], axis=0)
        return total.at[rows[:, 2]].add(contract(first, second))

    return lax.fori_loop(0, tasks.shape[0] // block, step, jnp.zeros(shape, jnp.float32))


def left_product(env_part, wave_part):
    return jnp.einsum("bij,bvjk->bvik", env_part, wave_part, preferred_element_type=jnp.float32)


def right_product(inter_part, env_part):
    return jnp.einsum("bvij,bjk->bvik", inter_part, env_part, preferred_element_type=jnp.float32)


def shards(wave_tiles, left_env, right_env, send_list, left_tasks, right_tasks):
    env_left, env_right = (
        lax.all_gather(left_env, "sector", axis=1, tiled=True),
        lax.all_gather(right_env, "sector", axis=1, tiled=True),
    )
    env_left = env_left[0]
    env_right = env_right[0]
    slot_list = send_list[0]
    live = slot_list >= 0
    picked = jnp.take(wave_tiles, jnp.maximum(slot_list, 0), axis=0)
    outgoing = jnp.where(live[:, None, None, None], picked, jnp.zeros((), jnp.bfloat16))
    tile_dim = wave_tiles.shape[2]
    groups = lax.axis_size("term")
    share = tile_dim // groups
    received = lax.all_to_all(outgoing, "sector", split_axis=0, concat_axis=0, tiled=True)
    inter = run_tasks(left_tasks[0, 0], env_left, received, left_product, INTER_TILES).astype(
        jnp.bfloat16
    )
    partial_value = run_tasks(
        right_tasks[0, 0], inter, env_right, right_product, wave_tiles.shape[0]
    )
    summed = lax.psum(partial_value, "term")
    return lax.dynamic_slice_in_dim(summed, lax.axis_index("term") * share, share, 2)


def solution(mesh):
    in_specs = (
        P("sector", None, None, None),
        P("term", "sector", None, None),
        P("term", "sector", None, None),
        P("sector", None),
        P("term", "sector", None, None),
        P("term", "sector", None, None),
    )
    out_specs = P("sector", None, "term", None)
    return jax.shard_map(shards, mesh=mesh, in_specs=in_specs, out_specs=out_specs, check_vma=False)
```

profile of v0, /device:TPU:2, one launch (start us, length us, event | category | flops | bytes accessed | tf_op | source)
XLA Modules:
  0.0 562.8 jit_solution(14975568767976974510)
XLA Ops:
  8.0 6.5 %gather_fusion.4 = bf16[128,2,128,128]{3,2,1,0:T(8,128)(2,1)} fusion(bf16[16,2,128,128]{3,2,1,0:T(8,128)(2,1)S(1)} %copy-done, s32[1024]{0:T(1024)S(1)} %pad_clamp_fusion.4), kind=kCustom, calls=%fused_computation.4 | custom fusion | bytes 16777728 | tf_op jit(solution)/shard_map/jit(_take)/gather | solution.py:40
  14.5 7.5 %select_select_fusion = bf16[128,2,128,128]{3,2,1,0:T(8,128)(2,1)} fusion(bf16[128,2,128,128]{3,2,1,0:T(8,128)(2,1)} %gather_fusion.4, pred[128]{0:T(512)(128)(4,1)S(1)} %get-tuple-element.225, pred[128]{0:T(512)(128)(4,1)S(1)} %get-tuple-element.224), kind=kLoop, calls=%fused_computation.45 | loop fusion | flops 8388608 | bytes 16777472 | tf_op jit(solution)/shard_map/jit(_where)/select_n | solution.py:41
  22.0 11.3 %all-to-all-start = ((bf16[128,2,128,128]{3,2,1,0:T(8,128)(2,1)}), bf16[128,2,128,128]{3,2,1,0:T(8,128)(2,1)}, u32[]{:S(2)}, u32[]{:S(2)}) async-start(bf16[128,2,128,128]{3,2,1,0:T(8,128)(2,1)} %select_select_fusion), calls=%async_computation | async-start | bytes 16777216 | tf_op jit(solution)/shard_map/all_to_all | solution.py:45
  34.8 102.3 %all-gather.3.cloned.1.call-done = bf16[1,64,128,128]{3,2,0,1:T(8,128)(2,1)} async-done(((bf16[1,1,128,128]{3,2,0,1:T(8,128)(2,1)}), bf16[1,64,128,128]{3,2,0,1:T(8,128)(2,1)}) %all-gather.3.cloned.1.call-update) | async-done | bytes 2097168 | tf_op jit(solution)/shard_map/all_gather | solution.py:33
  137.1 90.6 %all-to-all-done = bf16[128,2,128,128]{3,2,1,0:T(8,128)(2,1)} async-done(((bf16[128,2,128,128]{3,2,1,0:T(8,128)(2,1)}), bf16[128,2,128,128]{3,2,1,0:T(8,128)(2,1)}, u32[]{:S(2)}, u32[]{:S(2)}) %all-to-all-start) | async-done | bytes 8388640 | tf_op jit(solution)/shard_map/all_to_all | solution.py:45
  230.2 82.3 %while.26 = (s32[]{:T(128)}, f32[32,2,128,128]{3,2,1,0:T(8,128)}, s32[96,3]{0,1:T(4,128)S(1)}, bf16[128,2,128,128]{3,2,1,0:T(8,128)(2,1)}, bf16[64,128,128]{2,1,...) while((s32[]{:T(128)}, f32[32,2,128,128]{3,2,1,0:T(8,128)}, s32[96,3]{0,1:T(4,128)S(1)}, ...), condition=%wide.region_2.4_spmd, body=%wide.region_0.3_spmd.sunk | while | flops 271059520 | bytes 34613776 | solution.py:20
  230.3 4.4 gather_fusion
  242.1 5.6 copy.23
  247.7 10.1 %scatter_fusion = f32[32,2,128,128]{3,2,1,0:T(8,128)} fusion(f32[32,2,128,128]{3,2,1,0:T(8,128)} %get-tuple-element.314, s32[32]{0:T(128)S(1)} %get-tuple-element.291, f32[32,2,128,128]{3,2,1,0:T(8,128)} %copy.23), kind=kCustom, calls=%fused_computation.5.clone.1 | custom fusion | flops 1048576 | bytes 12583040 | tf_op jit(solution)/shard_map/while/body/eval_jaxpr/scatter-add | solution.py:18
  257.9 4.3 gather_fusion
  269.6 5.6 copy.23
  275.2 9.9 %scatter_fusion = f32[32,2,128,128]{3,2,1,0:T(8,128)} fusion(f32[32,2,128,128]{3,2,1,0:T(8,128)} %get-tuple-element.314, s32[32]{0:T(128)S(1)} %get-tuple-element.291, f32[32,2,128,128]{3,2,1,0:T(8,128)} %copy.23), kind=kCustom, calls=%fused_computation.5.clone.1 | custom fusion | flops 1048576 | bytes 12583040 | tf_op jit(solution)/shard_map/while/body/eval_jaxpr/scatter-add | solution.py:18
  296.9 5.6 copy.23
  302.6 9.9 %scatter_fusion = f32[32,2,128,128]{3,2,1,0:T(8,128)} fusion(f32[32,2,128,128]{3,2,1,0:T(8,128)} %get-tuple-element.314, s32[32]{0:T(128)S(1)} %get-tuple-element.291, f32[32,2,128,128]{3,2,1,0:T(8,128)} %copy.23), kind=kCustom, calls=%fused_computation.5.clone.1 | custom fusion | flops 1048576 | bytes 12583040 | tf_op jit(solution)/shard_map/while/body/eval_jaxpr/scatter-add | solution.py:18
  316.6 145.3 %while.27 = (s32[]{:T(128)}, f32[16,2,128,128]{3,2,1,0:T(8,128)S(1)}, s32[256,3]{0,1:T(4,128)S(1)}, bf16[32,2,128,128]{3,2,1,0:T(8,128)(2,1)}, bf16[64,128,128]{...) while((s32[]{:T(128)}, f32[16,2,128,128]{3,2,1,0:T(8,128)S(1)}, ...), condition=%wide.region_5.7_spmd, body=%wide.region_3.6_spmd.sunk | while | flops 271059520 | bytes 26225168 | solution.py:20
  323.7 4.6 fusion.34
  328.3 6.5 %scatter_fusion.1 = f32[16,2,128,128]{3,2,1,0:T(8,128)S(1)} fusion(f32[16,2,128,128]{3,2,1,0:T(8,128)S(1)} %get-tuple-element.341, s32[32]{0:T(128)S(1)} %get-tuple-element.300, f32[32,2,128,128]{3,2,1,0:T(8,128)} %fusion.34), kind=kCustom, calls=%fused_computation.6.clone.1 | custom fusion | flops 1048576 | bytes 12583040 | tf_op jit(solution)/shard_map/while/body/eval_jaxpr/scatter-add | solution.py:18
  341.9 4.6 fusion.34
  346.5 6.5 %scatter_fusion.1 = f32[16,2,128,128]{3,2,1,0:T(8,128)S(1)} fusion(f32[16,2,128,128]{3,2,1,0:T(8,128)S(1)} %get-tuple-element.341, s32[32]{0:T(128)S(1)} %get-tuple-element.300, f32[32,2,128,128]{3,2,1,0:T(8,128)} %fusion.34), kind=kCustom, calls=%fused_computation.6.clone.1 | custom fusion | flops 1048576 | bytes 12583040 | tf_op jit(solution)/shard_map/while/body/eval_jaxpr/scatter-add | solution.py:18
  360.0 4.6 fusion.34
  364.6 6.5 %scatter_fusion.1 = f32[16,2,128,128]{3,2,1,0:T(8,128)S(1)} fusion(f32[16,2,128,128]{3,2,1,0:T(8,128)S(1)} %get-tuple-element.341, s32[32]{0:T(128)S(1)} %get-tuple-element.300, f32[32,2,128,128]{3,2,1,0:T(8,128)} %fusion.34), kind=kCustom, calls=%fused_computation.6.clone.1 | custom fusion | flops 1048576 | bytes 12583040 | tf_op jit(solution)/shard_map/while/body/eval_jaxpr/scatter-add | solution.py:18
  378.2 4.6 fusion.34
  382.8 6.5 %scatter_fusion.1 = f32[16,2,128,128]{3,2,1,0:T(8,128)S(1)} fusion(f32[16,2,128,128]{3,2,1,0:T(8,128)S(1)} %get-tuple-element.341, s32[32]{0:T(128)S(1)} %get-tuple-element.300, f32[32,2,128,128]{3,2,1,0:T(8,128)} %fusion.34), kind=kCustom, calls=%fused_computation.6.clone.1 | custom fusion | flops 1048576 | bytes 12583040 | tf_op jit(solution)/shard_map/while/body/eval_jaxpr/scatter-add | solution.py:18
  396.4 4.6 fusion.34
  400.9 6.5 %scatter_fusion.1 = f32[16,2,128,128]{3,2,1,0:T(8,128)S(1)} fusion(f32[16,2,128,128]{3,2,1,0:T(8,128)S(1)} %get-tuple-element.341, s32[32]{0:T(128)S(1)} %get-tuple-element.300, f32[32,2,128,128]{3,2,1,0:T(8,128)} %fusion.34), kind=kCustom, calls=%fused_computation.6.clone.1 | custom fusion | flops 1048576 | bytes 12583040 | tf_op jit(solution)/shard_map/while/body/eval_jaxpr/scatter-add | solution.py:18
  414.5 4.6 fusion.34
  419.1 6.5 %scatter_fusion.1 = f32[16,2,128,128]{3,2,1,0:T(8,128)S(1)} fusion(f32[16,2,128,128]{3,2,1,0:T(8,128)S(1)} %get-tuple-element.341, s32[32]{0:T(128)S(1)} %get-tuple-element.300, f32[32,2,128,128]{3,2,1,0:T(8,128)} %fusion.34), kind=kCustom, calls=%fused_computation.6.clone.1 | custom fusion | flops 1048576 | bytes 12583040 | tf_op jit(solution)/shard_map/while/body/eval_jaxpr/scatter-add | solution.py:18
  432.7 4.6 fusion.34
  437.2 6.5 %scatter_fusion.1 = f32[16,2,128,128]{3,2,1,0:T(8,128)S(1)} fusion(f32[16,2,128,128]{3,2,1,0:T(8,128)S(1)} %get-tuple-element.341, s32[32]{0:T(128)S(1)} %get-tuple-element.300, f32[32,2,128,128]{3,2,1,0:T(8,128)} %fusion.34), kind=kCustom, calls=%fused_computation.6.clone.1 | custom fusion | flops 1048576 | bytes 12583040 | tf_op jit(solution)/shard_map/while/body/eval_jaxpr/scatter-add | solution.py:18
  450.8 4.6 fusion.34
  455.4 6.5 %scatter_fusion.1 = f32[16,2,128,128]{3,2,1,0:T(8,128)S(1)} fusion(f32[16,2,128,128]{3,2,1,0:T(8,128)S(1)} %get-tuple-element.341, s32[32]{0:T(128)S(1)} %get-tuple-element.300, f32[32,2,128,128]{3,2,1,0:T(8,128)} %fusion.34), kind=kCustom, calls=%fused_computation.6.clone.1 | custom fusion | flops 1048576 | bytes 12583040 | tf_op jit(solution)/shard_map/while/body/eval_jaxpr/scatter-add | solution.py:18
  463.2 91.4 %all-reduce.2.cloned.1.call-done = f32[16,2,128,128]{3,2,1,0:T(8,128)} async-done(((f32[16,2,128,128]{3,2,1,0:T(8,128)}), f32[16,2,128,128]{3,2,1,0:T(8,128)}) %all-reduce.2.cloned.1.call-update) | async-done | bytes 2097168 | tf_op jit(solution)/shard_map/psum | solution.py:52
  (113 shorter events, 95.7 us)
Async XLA Ops:
  6.5 1.4 copy-start
  22.0 12.8 %copy-start.3 = (s32[1,1,96,3]{2,1,3,0:T(1,128)S(1)}, s32[1,1,96,3]{2,1,3,0:T(1,128)}, u32[]{:S(2)}) copy-start(s32[1,1,96,3]{2,1,3,0:T(1,128)} %param.16) | copy-start | bytes 3460
  22.0 12.8 %copy-start.2 = (s32[1,1,256,3]{2,1,3,0:T(1,128)S(1)}, s32[1,1,256,3]{2,1,3,0:T(1,128)}, u32[]{:S(2)}) copy-start(s32[1,1,256,3]{2,1,3,0:T(1,128)} %param.17) | copy-start | bytes 9220
  22.0 205.8 %all-to-all-start = ((bf16[128,2,128,128]{3,2,1,0:T(8,128)(2,1)}), bf16[128,2,128,128]{3,2,1,0:T(8,128)(2,1)}, u32[]{:S(2)}, u32[]{:S(2)}) async-start(bf16[128,2,128,128]{3,2,1,0:T(8,128)(2,1)} %select_select_fusion), calls=%async_computation | async-start | bytes 16777216 | tf_op jit(solution)/shard_map/all_to_all | solution.py:45
  33.3 103.9 %all-gather.3.cloned.1.call-start = ((), (), s32[]{:S(2)}) async-start(), calls=%async_computation.1 | async-start | bytes 2129920 | tf_op jit(solution)/shard_map/all_gather | solution.py:33
  34.0 282.4 %all-gather.5.cloned.1.call-start = ((), (), s32[]{:S(2)}) async-start(), calls=%async_computation.2 | async-start | bytes 2129920 | tf_op jit(solution)/shard_map/all_gather | solution.py:34
  34.8 519.8 %all-reduce.2.cloned.1.call-start = ((), (), s32[]{:S(2)}) async-start(), calls=%async_computation.3 | async-start | bytes 4194304 | tf_op jit(solution)/shard_map/psum | solution.py:52
  461.9 1.3 copy-start.1
Sparse Core Ops, SparseCore 0:
  37.5 99.6 all-gather.2
  140.5 95.8 all-gather.4
  463.3 91.2 all-reduce.1
where the time goes:
time: 565 us; the launch traced here: 563 us
  waiting for transfers between devices  286 us (51%)
  local copies, waits for them, and re-layouts  109 us (19%)
  other arithmetic  95 us (17%)
  matrix products  48.7 us (9%)
  between operations  13.2 us (2%)
  starting transfers between devices  11.4 us (2%)
    all_gather x1, waiting for transfers between devices, shards(): lax.all_gather(left_env, 'sector', axis=1, tiled=True)  102 us
    psum x1, waiting for transfers between devices, shards(): summed = lax.psum(partial_value, 'term')  91.4 us
    all_to_all x1, waiting for transfers between devices, shards(): lax.all_to_all(outgoing, 'sector', split_axis=0, concat_axis=0, tiled=True)  90.6 us
    scatter-add x11, other arithmetic, step(): return total.at[rows[:, 2]].add(contract(first, second))  81.8 us
    gather x11, local copies, waits for them, and re-layouts, step(): first = jnp.take(first_tiles, rows[:, 0], axis=0)  39.8 us
    gather x11, local copies, waits for them, and re-layouts, step(): second = jnp.take(second_tiles, rows[:, 1], axis=0)  38.9 us
    dot_general x8, matrix products, right_product(): jnp.einsum('bvij,bjk->bvik', inter_part, env_part, preferred_element_type...  36.6 us
    transpose x3, local copies, waits for them, and re-layouts, left_product(): jnp.einsum('bij,bvjk->bvik', env_part, wave_part, preferred_element_type=...  16.9 us
  transfers between devices with their start and end apart: 4, of which 3 were waited for; matrix products, arithmetic and copies ran while one was open for 16% of the time, Pallas kernels for 0%

commit v1 on v0

--- a/solution.py
+++ b/solution.py
@@ -30,7 +30,9 @@
 
 def shards(wave_tiles, left_env, right_env, send_list, left_tasks, right_tasks):
     env_left, env_right = (
-        lax.all_gather(left_env, "sector", axis=1, tiled=True),
+        jnp.concatenate(
+            lax.all_to_all(jnp.stack([left_env] * lax.axis_size("sector")), "sector", 0, 0), axis=1
+        ),
         lax.all_gather(right_env, "sector", axis=1, tiled=True),
     )
     env_left = env_left[0]

time: 565 us -> 608 us (1.076)
  waiting for transfers between devices: 286 us -> 316 us
  starting transfers between devices: 11.4 us -> 18.6 us
    all_gather x1 -> x0, waiting for transfers between devices: 102 us -> none  [shards(): lax.all_gather(left_env, 'sector', axis=1, tiled=True)]
    all_to_all x1, waiting for transfers between devices: 90.6 us -> 189 us  [shards(): lax.all_to_all(outgoing, 'sector', split_axis=0, concat_axis=0, tiled=True)]
    all_to_all x0 -> x1, waiting for transfers between devices: none -> 35.4 us  [shards(): lax.all_to_all(jnp.stack([left_env] * lax.axis_size('sector')), 'sector',...]
    all_to_all x0 -> x1, starting transfers between devices: none -> 10.8 us  [shards(): lax.all_to_all(jnp.stack([left_env] * lax.axis_size('sector')), 'sector',...]
  transfers between devices with their start and end apart: 4 -> 4, of which waited for: 3 -> 3; matrix products, arithmetic and copies ran while one was open for 16% -> 17% of each run, Pallas kernels for 0% -> 0%
where the time goes in v1:
time: 608 us; the launch traced here: 606 us
  waiting for transfers between devices  316 us (52%)
  local copies, waits for them, and re-layouts  115 us (19%)
  other arithmetic  93.9 us (15%)
  matrix products  48.8 us (8%)
  starting transfers between devices  18.6 us (3%)
  between operations  13.5 us (2%)
    all_to_all x1, waiting for transfers between devices, shards(): lax.all_to_all(outgoing, 'sector', split_axis=0, concat_axis=0, tiled=True)  189 us
    psum x1, waiting for transfers between devices, shards(): summed = lax.psum(partial_value, 'term')  90.3 us
    scatter-add x11, other arithmetic, step(): return total.at[rows[:, 2]].add(contract(first, second))  82 us
    gather x11, local copies, waits for them, and re-layouts, step(): first = jnp.take(first_tiles, rows[:, 0], axis=0)  39.8 us
    gather x11, local copies, waits for them, and re-layouts, step(): second = jnp.take(second_tiles, rows[:, 1], axis=0)  38.9 us
    dot_general x8, matrix products, right_product(): jnp.einsum('bvij,bjk->bvik', inter_part, env_part, preferred_element_type...  36.7 us
    all_to_all x1, waiting for transfers between devices, shards(): lax.all_to_all(jnp.stack([left_env] * lax.axis_size('sector')), 'sector',...  35.4 us
    transpose x3, local copies, waits for them, and re-layouts, left_product(): jnp.einsum('bij,bvjk->bvik', env_part, wave_part, preferred_element_type=...  16.8 us
  transfers between devices with their start and end apart: 4, of which 3 were waited for; matrix products, arithmetic and copies ran while one was open for 17% of the time, Pallas kernels for 0%

profile of v1, /device:TPU:2, one launch (start us, length us, event | category | flops | bytes accessed | tf_op | source)
XLA Modules:
  0.0 605.8 jit_solution(13523660883666209258)
XLA Ops:
  9.2 10.8 %all-to-all-start.1 = ((bf16[64,1,1,128,128]{4,3,2,1,0:T(8,128)(2,1)}), bf16[64,1,1,128,128]{4,3,2,1,0:T(8,128)(2,1)S(1)}, u32[]{:S(2)}, u32[]{:S(2)}) async-start(bf16[64,1,1,128,128]{4,3,2,1,0:T(8,128)(2,1)} %stack.2), calls=%async_computation.1 | async-start | bytes 4194304 | tf_op jit(solution)/shard_map/all_to_all | solution.py:34
  20.1 6.5 %gather_fusion.4 = bf16[128,2,128,128]{3,2,1,0:T(8,128)(2,1)} fusion(bf16[16,2,128,128]{3,2,1,0:T(8,128)(2,1)S(1)} %copy-done, s32[1024]{0:T(1024)S(1)} %pad_clamp_fusion.4), kind=kCustom, calls=%fused_computation.4 | custom fusion | bytes 16777728 | tf_op jit(solution)/shard_map/jit(_take)/gather | solution.py:42
  26.6 7.5 %select_select_fusion = bf16[128,2,128,128]{3,2,1,0:T(8,128)(2,1)} fusion(bf16[128,2,128,128]{3,2,1,0:T(8,128)(2,1)} %gather_fusion.4, pred[128]{0:T(512)(128)(4,1)S(1)} %get-tuple-element.225, pred[128]{0:T(512)(128)(4,1)S(1)} %get-tuple-element.224), kind=kLoop, calls=%fused_computation.45 | loop fusion | flops 8388608 | bytes 16777472 | tf_op jit(solution)/shard_map/jit(_where)/select_n | solution.py:43
  34.1 35.4 %all-to-all-done.1 = bf16[64,1,1,128,128]{4,3,2,1,0:T(8,128)(2,1)S(1)} async-done(((bf16[64,1,1,128,128]{4,3,2,1,0:T(8,128)(2,1)}), bf16[64,1,1,128,128]{4,3,2,1,0:T(8,128)(2,1)S(1)}, u32[]{:S(2)}, u32[]{:S(2)}) %all-to-all-start.1) | async-done | bytes 2097184 | tf_op jit(solution)/shard_map/all_to_all | solution.py:34
  69.6 7.7 %all-to-all-start = ((bf16[128,2,128,128]{3,2,1,0:T(8,128)(2,1)}), bf16[128,2,128,128]{3,2,1,0:T(8,128)(2,1)}, u32[]{:S(2)}, u32[]{:S(2)}) async-start(bf16[128,2,128,128]{3,2,1,0:T(8,128)(2,1)} %select_select_fusion), calls=%async_computation | async-start | bytes 16777216 | tf_op jit(solution)/shard_map/all_to_all | solution.py:47
  78.1 189.3 %all-to-all-done = bf16[128,2,128,128]{3,2,1,0:T(8,128)(2,1)} async-done(((bf16[128,2,128,128]{3,2,1,0:T(8,128)(2,1)}), bf16[128,2,128,128]{3,2,1,0:T(8,128)(2,1)}, u32[]{:S(2)}, u32[]{:S(2)}) %all-to-all-start) | async-done | bytes 8388640 | tf_op jit(solution)/shard_map/all_to_all | solution.py:47
  269.9 86.2 %while.26 = (s32[]{:T(128)}, f32[32,2,128,128]{3,2,1,0:T(8,128)}, s32[96,3]{0,1:T(4,128)S(1)}, bf16[128,2,128,128]{3,2,1,0:T(8,128)(2,1)}, bf16[64,128,128]{2,1,...) while((s32[]{:T(128)}, f32[32,2,128,128]{3,2,1,0:T(8,128)}, s32[96,3]{0,1:T(4,128)S(1)}, ...), condition=%wide.region_2.4_spmd, body=%wide.region_0.3_spmd.sunk | while | flops 271059520 | bytes 51391044 | solution.py:20
  271.2 4.3 gather_fusion
  282.9 5.6 copy.22
  288.6 10.2 %scatter_fusion = f32[32,2,128,128]{3,2,1,0:T(8,128)} fusion(f32[32,2,128,128]{3,2,1,0:T(8,128)} %get-tuple-element.314, s32[32]{0:T(128)S(1)} %get-tuple-element.291, f32[32,2,128,128]{3,2,1,0:T(8,128)} %copy.22), kind=kCustom, calls=%fused_computation.5.clone.1 | custom fusion | flops 1048576 | bytes 12583040 | tf_op jit(solution)/shard_map/while/body/eval_jaxpr/scatter-add | solution.py:18
  311.8 5.6 copy.22
  317.4 10.0 %scatter_fusion = f32[32,2,128,128]{3,2,1,0:T(8,128)} fusion(f32[32,2,128,128]{3,2,1,0:T(8,128)} %get-tuple-element.314, s32[32]{0:T(128)S(1)} %get-tuple-element.291, f32[32,2,128,128]{3,2,1,0:T(8,128)} %copy.22), kind=kCustom, calls=%fused_computation.5.clone.1 | custom fusion | flops 1048576 | bytes 12583040 | tf_op jit(solution)/shard_map/while/body/eval_jaxpr/scatter-add | solution.py:18
  340.5 5.6 copy.22
  346.1 10.0 %scatter_fusion = f32[32,2,128,128]{3,2,1,0:T(8,128)} fusion(f32[32,2,128,128]{3,2,1,0:T(8,128)} %get-tuple-element.314, s32[32]{0:T(128)S(1)} %get-tuple-element.291, f32[32,2,128,128]{3,2,1,0:T(8,128)} %copy.22), kind=kCustom, calls=%fused_computation.5.clone.1 | custom fusion | flops 1048576 | bytes 12583040 | tf_op jit(solution)/shard_map/while/body/eval_jaxpr/scatter-add | solution.py:18
  360.2 145.5 %while.27 = (s32[]{:T(128)}, f32[16,2,128,128]{3,2,1,0:T(8,128)S(1)}, s32[256,3]{0,1:T(4,128)S(1)}, bf16[32,2,128,128]{3,2,1,0:T(8,128)(2,1)}, bf16[64,128,128]{...) while((s32[]{:T(128)}, f32[16,2,128,128]{3,2,1,0:T(8,128)S(1)}, ...), condition=%wide.region_5.7_spmd, body=%wide.region_3.6_spmd.sunk | while | flops 271059520 | bytes 26225168 | solution.py:20
  367.3 4.6 fusion.34
  371.9 6.5 %scatter_fusion.1 = f32[16,2,128,128]{3,2,1,0:T(8,128)S(1)} fusion(f32[16,2,128,128]{3,2,1,0:T(8,128)S(1)} %get-tuple-element.341, s32[32]{0:T(128)S(1)} %get-tuple-element.300, f32[32,2,128,128]{3,2,1,0:T(8,128)} %fusion.34), kind=kCustom, calls=%fused_computation.6.clone.1 | custom fusion | flops 1048576 | bytes 12583040 | tf_op jit(solution)/shard_map/while/body/eval_jaxpr/scatter-add | solution.py:18
  385.5 4.6 fusion.34
  390.1 6.5 %scatter_fusion.1 = f32[16,2,128,128]{3,2,1,0:T(8,128)S(1)} fusion(f32[16,2,128,128]{3,2,1,0:T(8,128)S(1)} %get-tuple-element.341, s32[32]{0:T(128)S(1)} %get-tuple-element.300, f32[32,2,128,128]{3,2,1,0:T(8,128)} %fusion.34), kind=kCustom, calls=%fused_computation.6.clone.1 | custom fusion | flops 1048576 | bytes 12583040 | tf_op jit(solution)/shard_map/while/body/eval_jaxpr/scatter-add | solution.py:18
  403.7 4.6 fusion.34
  408.3 6.5 %scatter_fusion.1 = f32[16,2,128,128]{3,2,1,0:T(8,128)S(1)} fusion(f32[16,2,128,128]{3,2,1,0:T(8,128)S(1)} %get-tuple-element.341, s32[32]{0:T(128)S(1)} %get-tuple-element.300, f32[32,2,128,128]{3,2,1,0:T(8,128)} %fusion.34), kind=kCustom, calls=%fused_computation.6.clone.1 | custom fusion | flops 1048576 | bytes 12583040 | tf_op jit(solution)/shard_map/while/body/eval_jaxpr/scatter-add | solution.py:18
  421.9 4.6 fusion.34
  426.5 6.5 %scatter_fusion.1 = f32[16,2,128,128]{3,2,1,0:T(8,128)S(1)} fusion(f32[16,2,128,128]{3,2,1,0:T(8,128)S(1)} %get-tuple-element.341, s32[32]{0:T(128)S(1)} %get-tuple-element.300, f32[32,2,128,128]{3,2,1,0:T(8,128)} %fusion.34), kind=kCustom, calls=%fused_computation.6.clone.1 | custom fusion | flops 1048576 | bytes 12583040 | tf_op jit(solution)/shard_map/while/body/eval_jaxpr/scatter-add | solution.py:18
  440.1 4.6 fusion.34
  444.7 6.5 %scatter_fusion.1 = f32[16,2,128,128]{3,2,1,0:T(8,128)S(1)} fusion(f32[16,2,128,128]{3,2,1,0:T(8,128)S(1)} %get-tuple-element.341, s32[32]{0:T(128)S(1)} %get-tuple-element.300, f32[32,2,128,128]{3,2,1,0:T(8,128)} %fusion.34), kind=kCustom, calls=%fused_computation.6.clone.1 | custom fusion | flops 1048576 | bytes 12583040 | tf_op jit(solution)/shard_map/while/body/eval_jaxpr/scatter-add | solution.py:18
  458.3 4.6 fusion.34
  462.9 6.5 %scatter_fusion.1 = f32[16,2,128,128]{3,2,1,0:T(8,128)S(1)} fusion(f32[16,2,128,128]{3,2,1,0:T(8,128)S(1)} %get-tuple-element.341, s32[32]{0:T(128)S(1)} %get-tuple-element.300, f32[32,2,128,128]{3,2,1,0:T(8,128)} %fusion.34), kind=kCustom, calls=%fused_computation.6.clone.1 | custom fusion | flops 1048576 | bytes 12583040 | tf_op jit(solution)/shard_map/while/body/eval_jaxpr/scatter-add | solution.py:18
  476.5 4.6 fusion.34
  481.0 6.5 %scatter_fusion.1 = f32[16,2,128,128]{3,2,1,0:T(8,128)S(1)} fusion(f32[16,2,128,128]{3,2,1,0:T(8,128)S(1)} %get-tuple-element.341, s32[32]{0:T(128)S(1)} %get-tuple-element.300, f32[32,2,128,128]{3,2,1,0:T(8,128)} %fusion.34), kind=kCustom, calls=%fused_computation.6.clone.1 | custom fusion | flops 1048576 | bytes 12583040 | tf_op jit(solution)/shard_map/while/body/eval_jaxpr/scatter-add | solution.py:18
  494.6 4.6 fusion.34
  499.2 6.5 %scatter_fusion.1 = f32[16,2,128,128]{3,2,1,0:T(8,128)S(1)} fusion(f32[16,2,128,128]{3,2,1,0:T(8,128)S(1)} %get-tuple-element.341, s32[32]{0:T(128)S(1)} %get-tuple-element.300, f32[32,2,128,128]{3,2,1,0:T(8,128)} %fusion.34), kind=kCustom, calls=%fused_computation.6.clone.1 | custom fusion | flops 1048576 | bytes 12583040 | tf_op jit(solution)/shard_map/while/body/eval_jaxpr/scatter-add | solution.py:18
  507.1 90.3 %all-reduce.2.cloned.1.call-done = f32[16,2,128,128]{3,2,1,0:T(8,128)} async-done(((f32[16,2,128,128]{3,2,1,0:T(8,128)}), f32[16,2,128,128]{3,2,1,0:T(8,128)}) %all-reduce.2.cloned.1.call-update) | async-done | bytes 2097168 | tf_op jit(solution)/shard_map/psum | solution.py:54
  (127 shorter events, 104.5 us)
Async XLA Ops:
  6.5 13.5 %copy-start = (bf16[16,2,128,128]{3,2,1,0:T(8,128)(2,1)S(1)}, bf16[16,2,128,128]{3,2,1,0:T(8,128)(2,1)}, u32[]{:S(2)}) copy-start(bf16[16,2,128,128]{3,2,1,0:T(8,128)(2,1)} %param.12) | copy-start | bytes 3145732
  9.2 10.8 %copy-start.6 = (s32[1,128]{1,0:T(1,128)S(1)}, s32[1,128]{1,0:T(1,128)}, u32[]{:S(2)}) copy-start(s32[1,128]{1,0:T(1,128)} %param.15) | copy-start | bytes 1540
  9.2 60.3 %all-to-all-start.1 = ((bf16[64,1,1,128,128]{4,3,2,1,0:T(8,128)(2,1)}), bf16[64,1,1,128,128]{4,3,2,1,0:T(8,128)(2,1)S(1)}, u32[]{:S(2)}, u32[]{:S(2)}) async-start(bf16[64,1,1,128,128]{4,3,2,1,0:T(8,128)(2,1)} %stack.2), calls=%async_computation.1 | async-start | bytes 4194304 | tf_op jit(solution)/shard_map/all_to_all | solution.py:34
  34.1 44.0 %copy-start.5 = (s32[1,1,96,3]{2,1,3,0:T(1,128)S(1)}, s32[1,1,96,3]{2,1,3,0:T(1,128)}, u32[]{:S(2)}) copy-start(s32[1,1,96,3]{2,1,3,0:T(1,128)} %param.16) | copy-start | bytes 3460
  34.1 44.0 %copy-start.4 = (s32[1,1,256,3]{2,1,3,0:T(1,128)S(1)}, s32[1,1,256,3]{2,1,3,0:T(1,128)}, u32[]{:S(2)}) copy-start(s32[1,1,256,3]{2,1,3,0:T(1,128)} %param.17) | copy-start | bytes 9220
  69.6 197.9 %all-to-all-start = ((bf16[128,2,128,128]{3,2,1,0:T(8,128)(2,1)}), bf16[128,2,128,128]{3,2,1,0:T(8,128)(2,1)}, u32[]{:S(2)}, u32[]{:S(2)}) async-start(bf16[128,2,128,128]{3,2,1,0:T(8,128)(2,1)} %select_select_fusion), calls=%async_computation | async-start | bytes 16777216 | tf_op jit(solution)/shard_map/all_to_all | solution.py:47
  77.3 282.7 %all-gather.2.cloned.1.call-start = ((), (), s32[]{:S(2)}) async-start(), calls=%async_computation.2 | async-start | bytes 2129920 | tf_op jit(solution)/shard_map/all_gather | solution.py:36
  78.0 519.3 %all-reduce.2.cloned.1.call-start = ((), (), s32[]{:S(2)}) async-start(), calls=%async_computation.3 | async-start | bytes 4194304 | tf_op jit(solution)/shard_map/psum | solution.py:54
  269.9 1.3 copy-start.2
  288.6 10.2 %copy-start.3 = (bf16[64,128,128]{2,1,0:T(8,128)(2,1)S(1)}, bf16[64,128,128]{2,1,0:T(8,128)(2,1)}, u32[]{:S(2)}) copy-start(bf16[64,128,128]{2,1,0:T(8,128)(2,1)} %copy-done.2) | copy-start | bytes 6291460 | tf_op jit(solution)/shard_map/while
  298.7 1.3 copy-start.2
  317.4 10.0 %copy-start.3 = (bf16[64,128,128]{2,1,0:T(8,128)(2,1)S(1)}, bf16[64,128,128]{2,1,0:T(8,128)(2,1)}, u32[]{:S(2)}) copy-start(bf16[64,128,128]{2,1,0:T(8,128)(2,1)} %copy-done.2) | copy-start | bytes 6291460 | tf_op jit(solution)/shard_map/while
  327.4 1.3 copy-start.2
  346.1 10.0 %copy-start.3 = (bf16[64,128,128]{2,1,0:T(8,128)(2,1)S(1)}, bf16[64,128,128]{2,1,0:T(8,128)(2,1)}, u32[]{:S(2)}) copy-start(bf16[64,128,128]{2,1,0:T(8,128)(2,1)} %copy-done.2) | copy-start | bytes 6291460 | tf_op jit(solution)/shard_map/while
  505.7 1.3 copy-start.1
Sparse Core Ops, SparseCore 0:
  81.5 99.7 all-gather.1
  507.2 90.0 all-reduce.1
